TPU v7x, 512 devices: a whole 4x4x16 slice. The times are simulated.
512 devices in a mesh: dp: 16 (over z), expert: 32 (over y, x, core).
Axes of the slice: x: 4, y: 4, z: 16, core: 2. Of those that a mesh axis runs over, the one named last changes fastest.
Arguments:
- tokens: bfloat16 [2048, 4096], P('dp', 'expert'), may hold values from -6 to 6
- norm_gain: float32 [4096], replicated, may hold values from 0.1 to 1.9
- routes: int32 [2048, 2], P('dp'), may hold values from 0 to 31, all different within a row; in each aligned block of 128 rows (0 to 127, 128 to 255, ...) at most 10 rows name the same one
- route_prob: float32 [2048, 2], P('dp'), may hold values from 0.2 to 1
- gate_weight: bfloat16 [32, 4096, 2048], P('expert', None, 'dp'), may hold values from -0.09375 to 0.09375
- up_weight: bfloat16 [32, 4096, 2048], P('expert', None, 'dp'), may hold values from -0.09375 to 0.09375
- down_weight: bfloat16 [32, 2048, 4096], P('expert', 'dp'), may hold values from -0.125 to 0.125
- key_value_weight: bfloat16 [4096, 2048], P('expert'), may hold values from -0.09375 to 0.09375
- key_value_target: bfloat16 [2048, 2048], P('dp', 'expert'), may hold values from -6 to 6
- concept_mask: int32 [2048], P('dp'), may hold values 0 or 1
Outputs:
- down_grad: bfloat16 [32, 2048, 4096], P('expert', 'dp')
- key_value_grad: float32 [4096, 2048], P('expert', 'dp')
Inputs may be any that keep to these rules, and one draw needn't show every extreme that they name: `routes`: in each aligned block of 128 rows no expert is named by more than 10 rows; the two choices of a token differ.
All inputs are finite; a program needn't handle non-finite values. No bound on the sum of `concept_mask` on one device may be relied on, other than what follows from the above.
Results may differ from a plain program's by a relative error of at most 0.033.
Values may be sent and summed in bfloat16 or wider, within the bound.
No kernel may reach another device: no remote copies, remote signals or barrier semaphores. Data moves between devices by JAX's collectives and lax.ppermute only.
A program may use at most 64 MiB of HBM per device.

v0:
```python
import jax
import jax.numpy as jnp
from jax import lax
from jax.sharding import PartitionSpec as P

eps_norm = 1e-06


def slot_targets(routes, expert_count, capacity):
    flat = routes.reshape(-1)
    onehot = (flat[:, None] == jnp.arange(expert_count, dtype=jnp.int32)[None, :]).astype(jnp.int32)
    before = jnp.cumsum(onehot, axis=0) - onehot
    return flat * capacity + jnp.sum(before * onehot, axis=1)


def per_device(
    tokens,
    norm_gain,
    routes,
    route_prob,
    gate_weight,
    up_weight,
    down_weight,
    key_value_weight,
    key_value_target,
    concept_mask,
):
    token_rows, width = tokens.shape
    top_count = routes.shape[1]
    expert_count = lax.axis_size("expert")
    capacity = 5 * token_rows * top_count // (4 * expert_count)
    model_width = width * expert_count
    position = slot_targets(routes, expert_count, capacity)
    prob_flat = route_prob.reshape(-1)

    def place_rows(pair_rows):
        filled = (
            jnp.zeros((expert_count * capacity, width), jnp.bfloat16).at[position].set(pair_rows)
        )
        return filled.reshape(expert_count, capacity, width)

    values = tokens.astype(jnp.float32)
    total_sq = lax.psum(jnp.sum(values * values, axis=1), "expert")
    scale = lax.rsqrt(total_sq / model_width + eps_norm)
    local_gain = lax.dynamic_slice_in_dim(norm_gain, lax.axis_index("expert") * width, width)
    outgoing = (values * scale[:, None] * local_gain[None, :]).astype(jnp.bfloat16)
    send_slots = place_rows(jnp.repeat(outgoing, top_count, axis=0))
    arrived = lax.all_to_all(send_slots, "expert", split_axis=0, concat_axis=2, tiled=True)[0]
    rows = lax.all_gather(arrived, "dp", axis=0, tiled=True)
    gate_val = jnp.dot(rows, gate_weight[0], preferred_element_type=jnp.float32)
    up_val = jnp.dot(rows, up_weight[0], preferred_element_type=jnp.float32)
    hidden = (jax.nn.silu(gate_val) * up_val).astype(jnp.bfloat16)
    expert_out = lax.psum_scatter(
        jnp.dot(hidden, down_weight[0], preferred_element_type=jnp.float32).astype(jnp.bfloat16),
        "dp",
        scatter_dimension=0,
        tiled=True,
    )
    returned = lax.all_to_all(expert_out[None], "expert", split_axis=2, concat_axis=0, tiled=True)
    picked = returned.reshape(expert_count * capacity, width)[position].astype(jnp.float32)
    expert_mix = (picked * prob_flat[:, None]).reshape(token_rows, top_count, width).sum(axis=1)
    state = (tokens.astype(jnp.float32) + expert_mix).astype(jnp.bfloat16)
    proj_term = jnp.dot(state, key_value_weight, preferred_element_type=jnp.float32)
    proj_cols = lax.psum_scatter(
        proj_term.astype(jnp.bfloat16), "expert", scatter_dimension=1, tiled=True
    ).astype(jnp.float32)
    mask_col = concept_mask.astype(jnp.float32)[:, None]
    cotangent_cols = (
        mask_col * (proj_cols - key_value_target.astype(jnp.float32)) * token_rows ** (-0.5)
    ).astype(jnp.bfloat16)
    cotangent = lax.all_gather(cotangent_cols, "expert", axis=1, tiled=True)
    grad_term = jnp.einsum("tw,tk->wk", state, cotangent, preferred_element_type=jnp.float32)
    key_value_grad = lax.psum_scatter(
        grad_term.astype(jnp.bfloat16), "dp", scatter_dimension=1, tiled=True
    ).astype(jnp.float32)
    state_grad = jnp.einsum(
        "tk,wk->tw", cotangent, key_value_weight, preferred_element_type=jnp.float32
    )
    pair_grad = (jnp.repeat(state_grad, top_count, axis=0) * prob_flat[:, None]).astype(
        jnp.bfloat16
    )
    grad_slots = place_rows(pair_grad)
    landed = lax.all_to_all(grad_slots, "expert", split_axis=0, concat_axis=2, tiled=True)[0]
    down_total = jnp.einsum(
        "rf,rd->fd",
        hidden,
        lax.all_gather(landed, "dp", axis=0, tiled=True),
        preferred_element_type=jnp.float32,
    )
    return (down_total.astype(jnp.bfloat16)[None], key_value_grad)


def solution(mesh):
    placed = (
        P("dp", "expert"),
        P(),
        P("dp", None),
        P("dp", None),
        P("expert", None, "dp"),
        P("expert", None, "dp"),
        P("expert", "dp", None),
        P("expert", None),
        P("dp", "expert"),
        P("dp"),
    )
    return jax.shard_map(
        per_device,
        mesh=mesh,
        in_specs=placed,
        out_specs=(P("expert", "dp", None), P("expert", "dp")),
        check_vma=False,
    )
```

profile of v0, /device:TPU:2, one launch (start us, length us, event | category | flops | bytes accessed | tf_op | source)
XLA Modules:
  0.0 632.4 jit_solution(2933031377896465025)
XLA Ops:
  7.2 0.0 copy-start
  7.2 0.0 all-gather.5.cloned.1.call-start
  7.2 0.8 broadcast_multiply_fusion
  8.0 0.8 copy.34
  8.8 0.1 eq.29
  8.9 0.1 eq.25
  9.1 0.9 fusion.7
  9.9 63.0 %psum.7 = f32[128]{0:T(128)S(1)} all-reduce(f32[128]{0:T(128)S(1)} %fusion.7), channel_id=1, replica_groups=mesh['dp'=16,'expert'=32] {'expert'}, use_global_device_ids=true, to_apply=%region_4.5 | all-reduce | flops 128 | bytes 1024 | tf_op jit(solution)/shard_map/psum | solution.py:43
  72.9 0.1 copy.33
  73.0 0.1 mul.83
  73.2 0.6 reduce-window.6
  73.8 0.2 slice_reduce_fusion
  74.0 0.8 dynamic_slice.3
  74.8 0.8 fusion.9
  75.6 0.1 fusion.18
  75.8 1.2 scatter_custom_fusion
  77.0 14.9 %all_to_all.45 = bf16[32,10,128]{2,1,0:T(8,128)(2,1)S(1)} all-to-all(bf16[32,10,128]{2,1,0:T(8,128)(2,1)S(1)} %reshape.83), channel_id=1, replica_groups=mesh['dp'=16,'expert'=32] {'expert'}, dimensions={0} | all-to-all | bytes 163840 | tf_op jit(solution)/shard_map/all_to_all | solution.py:48
  92.0 0.7 reshape.112
  92.7 0.0 all-gather.5.cloned.1.call-update
  92.7 0.0 all-reduce.3.cloned.1.call-start
  92.8 74.1 %all-gather.5.cloned.1.call-done = bf16[16,10,4096]{2,1,0:T(8,128)(2,1)} async-done(((bf16[1,10,4096]{2,1,0:T(8,128)(2,1)}), bf16[16,10,4096]{2,1,0:T(8,128)(2,1)}) %all-gather.5.cloned.1.call-update) | async-done | bytes 1310736 | tf_op jit(solution)/shard_map/all_gather | solution.py:49
  166.9 1.8 reshape.113
  168.7 0.5 fusion.4
  169.2 0.7 copy-done.3
  170.0 0.5 fusion.1
  170.5 1.6 convolution_convert_fusion
  172.1 0.0 all-reduce.3.cloned.1.call-update
  172.1 0.1 copy.41
  172.2 1.3 dynamic-slice
  174.1 135.3 %all-reduce.3.cloned.1.call-done = bf16[160,4096]{1,0:T(8,128)(2,1)} async-done(((bf16[160,4096]{1,0:T(8,128)(2,1)}), bf16[160,4096]{1,0:T(8,128)(2,1)}) %all-reduce.3.cloned.1.call-update) | async-done | bytes 1310736
  309.4 1.0 dynamic-slice_bitcast_fusion
  310.4 2.8 copy.38
  313.2 0.5 broadcast.74
  313.7 23.4 %reduce.2 = bf16[4096,10]{1,0:T(8,128)(2,1)} reduce(bf16[4096,1,10]{2,1,0:T(2,128)(2,1)S(1)} %bitcast.74, bf16[]{:T(256)} %broadcast.74), dimensions={1}, to_apply=%bitcast.60.reduce_sub_computation | reduce | bytes 163842
  337.1 3.4 reshape.126
  340.5 7.4 %all-to-all-start.1 = ((bf16[32,2,640]{2,1,0:T(2,128)(2,1)}), bf16[32,2,640]{2,1,0:T(2,128)(2,1)S(1)}, u32[]{:S(2)}, u32[]{:S(2)}) async-start(bf16[32,2,640]{2,1,0:T(2,128)(2,1)} %reshape.126), calls=%async_computation.1 | async-start | bytes 163840 | tf_op jit(solution)/shard_map/all_to_all | solution.py:59
  348.0 0.0 reduce-scatter.5.cloned.1.call-start
  348.0 6.3 all-to-all-done.1
  354.3 2.2 reshape.127
  356.6 2.1 copy.39
  358.9 0.9 gather_fusion
  359.7 0.2 fusion.6
  360.0 1.1 convolution_convert_fusion.3
  361.1 0.0 reduce-scatter.5.cloned.1.call-update
  361.2 0.0 reduce-scatter.7.cloned.1.call-start
  361.2 93.7 %reduce-scatter.5.cloned.1.call-done = bf16[128,64]{0,1:T(8,128)(2,1)} async-done(((bf16[128,2048]{0,1:T(8,128)(2,1)}), bf16[128,64]{0,1:T(8,128)(2,1)}) %reduce-scatter.5.cloned.1.call-update) | async-done | bytes 16400 | tf_op jit(solution)/shard_map/reduce_scatter | solution.py:64
  455.0 0.7 multiply_convert_fusion.2
  455.7 23.2 %all_gather.10 = bf16[128,2048]{0,1:T(8,128)(2,1)S(1)} all-gather(bf16[128,64]{0,1:T(8,128)(2,1)S(1)} %multiply_convert_fusion.2), channel_id=1, replica_groups=mesh['dp'=16,'expert'=32] {'expert'}, dimensions={1}, use_global_device_ids=true | all-gather | bytes 540672 | tf_op jit(solution)/shard_map/all_gather | solution.py:71
  478.9 0.3 convolution_convert_fusion.2
  479.2 1.0 copy.44
  480.2 0.0 reduce-scatter.7.cloned.1.call-update
  480.2 0.0 all-gather.7.cloned.1.call-start
  480.3 0.1 mul.99
  480.4 0.3 fusion.22
  480.8 1.3 scatter_custom_fusion.1
  482.1 12.6 %all_to_all.46 = bf16[32,10,128]{2,1,0:T(8,128)(2,1)S(1)} all-to-all(bf16[32,10,128]{2,1,0:T(8,128)(2,1)S(1)} %reshape.86), channel_id=1, replica_groups=mesh['dp'=16,'expert'=32] {'expert'}, dimensions={0} | all-to-all | bytes 163840 | tf_op jit(solution)/shard_map/all_to_all | solution.py:83
  494.7 0.7 reshape.114
  495.4 0.0 all-gather.7.cloned.1.call-update
  495.4 54.2 %reduce-scatter.7.cloned.1.call-done = bf16[128,128]{1,0:T(8,128)(2,1)} async-done(((bf16[2048,128]{1,0:T(8,128)(2,1)}), bf16[128,128]{1,0:T(8,128)(2,1)}) %reduce-scatter.7.cloned.1.call-update) | async-done | bytes 32784
  549.6 0.9 copy.45
  550.5 0.6 convert_element_type.74
  551.1 71.5 %all-gather.7.cloned.1.call-done = bf16[16,10,4096]{2,1,0:T(8,128)(2,1)} async-done(((bf16[1,10,4096]{2,1,0:T(8,128)(2,1)}), bf16[16,10,4096]{2,1,0:T(8,128)(2,1)}) %all-gather.7.cloned.1.call-update) | async-done | bytes 1310736 | tf_op jit(solution)/shard_map/all_gather | solution.py:87
  622.7 1.8 reshape.115
  624.5 1.4 fusion
  (31 shorter events, 0.4 us)
Async XLA Ops:
  7.2 163.3 %copy-start = (bf16[1,128,4096]{2,1,0:T(8,128)(2,1)S(1)}, bf16[1,128,4096]{2,1,0:T(8,128)(2,1)}, u32[]{:S(2)}) copy-start(bf16[1,128,4096]{2,1,0:T(8,128)(2,1)} %param.16) | copy-start | bytes 3145732
  7.2 159.7 %all-gather.5.cloned.1.call-start = ((), (), s32[]{:S(2)}) async-start(), calls=%async_computation.6 | async-start | bytes 2228224 | tf_op jit(solution)/shard_map/all_gather | solution.py:49
  92.7 76.0 %copy-start.2 = (bf16[1,4096,128]{2,1,0:T(8,128)(2,1)S(1)}, bf16[1,4096,128]{2,1,0:T(8,128)(2,1)}, u32[]{:S(2)}) copy-start(bf16[1,4096,128]{2,1,0:T(8,128)(2,1)} %param.14) | copy-start | bytes 3145732
  92.7 216.7 %all-reduce.3.cloned.1.call-start = ((), (), s32[]{:S(2)}) async-start(), calls=%async_computation.9 | async-start | bytes 2621440
  168.7 1.2 copy-start.3
  170.5 1.6 copy-start.6
  340.5 13.8 %all-to-all-start.1 = ((bf16[32,2,640]{2,1,0:T(2,128)(2,1)}), bf16[32,2,640]{2,1,0:T(2,128)(2,1)S(1)}, u32[]{:S(2)}, u32[]{:S(2)}) async-start(bf16[32,2,640]{2,1,0:T(2,128)(2,1)} %reshape.126), calls=%async_computation.1 | async-start | bytes 163840 | tf_op jit(solution)/shard_map/all_to_all | solution.py:59
  348.0 107.0 %reduce-scatter.5.cloned.1.call-start = ((), (), s32[]{:S(2)}) async-start(), calls=%async_computation.5 | async-start | bytes 540672 | tf_op jit(solution)/shard_map/reduce_scatter | solution.py:64
  358.7 1.3 copy-start.1
  358.7 1.3 copy-start.4
  358.8 2.4 copy-start.7
  358.8 96.2 %copy-start.5 = (bf16[128,64]{0,1:T(8,128)(2,1)S(1)}, bf16[128,64]{0,1:T(8,128)(2,1)}, u32[]{:S(2)}) copy-start(bf16[128,64]{0,1:T(8,128)(2,1)} %param.18) | copy-start | bytes 49156
  361.2 188.5 %reduce-scatter.7.cloned.1.call-start = ((), (), s32[]{:S(2)}) async-start(), calls=%async_computation.8 | async-start | bytes 557056
  480.2 142.4 %all-gather.7.cloned.1.call-start = ((), (), s32[]{:S(2)}) async-start(), calls=%async_computation.7 | async-start | bytes 2228224 | tf_op jit(solution)/shard_map/all_gather | solution.py:87
Sparse Core Ops, SparseCore 0:
  92.8 74.0 all-gather.4
  172.2 137.1 all-reduce.2
  361.3 93.6 reduce-scatter.4
  480.3 69.2 reduce-scatter.6
  551.8 70.8 all-gather.6
where the time goes:
time: 633 us; the launch traced here: 632 us
  waiting for transfers between devices  435 us (69%)
  blocking collectives  114 us (18%)
  other arithmetic  29.5 us (5%)
  local copies, waits for them, and re-layouts  25.8 us (4%)
  between operations  14.8 us (2%)
  starting transfers between devices  7.63 us (1%)
    unnamed x7, waiting for transfers between devices  190 us
    reduce_scatter x1, waiting for transfers between devices, per_device(): lax.psum_scatter(proj_term.astype(jnp.bfloat16), 'expert', scatter_dimens...  93.7 us
    all_gather x1, waiting for transfers between devices, per_device(): rows = lax.all_gather(arrived, 'dp', axis=0, tiled=True)  74.1 us
    all_gather x1, waiting for transfers between devices, per_device(): lax.all_gather(landed, 'dp', axis=0, tiled=True)  71.5 us
    psum x1, blocking collectives, per_device(): total_sq = lax.psum(jnp.sum(values * values, axis=1), 'expert')  63 us
    unnamed x1, other arithmetic  23.4 us
    all_gather x1, blocking collectives, per_device(): cotangent = lax.all_gather(cotangent_cols, 'expert', axis=1, tiled=True)  23.2 us
    unnamed x29, local copies, waits for them, and re-layouts  16 us
  transfers between devices with their start and end apart: 6, of which 6 were waited for; matrix products, arithmetic and copies ran while one was open for 1% of the time, Pallas kernels for 0%

commit v1 on v0

--- a/solution.py
+++ b/solution.py
@@ -81,12 +81,37 @@
     )
     grad_slots = place_rows(pair_grad)
     landed = lax.all_to_all(grad_slots, "expert", split_axis=0, concat_axis=2, tiled=True)[0]
+    size, position_2, span = (lax.axis_size("dp"), lax.axis_index("dp"), landed.shape[0])
+    upward = [(i, (i + 1) % size) for i in range(size)]
+    downward = [(i, (i - 1) % size) for i in range(size)]
+    half = size // 2
+    from_left = from_right = landed
     down_total = jnp.einsum(
         "rf,rd->fd",
-        hidden,
-        lax.all_gather(landed, "dp", axis=0, tiled=True),
+        lax.dynamic_slice_in_dim(hidden, position_2 * span, landed.shape[0], axis=0),
+        landed,
         preferred_element_type=jnp.float32,
     )
+    for step in range(1, half + 1):
+        from_left = lax.ppermute(from_left, "dp", upward)
+        if step < size - half:
+            from_right = lax.ppermute(from_right, "dp", downward)
+            down_total = down_total + jnp.einsum(
+                "rf,rd->fd",
+                lax.dynamic_slice_in_dim(
+                    hidden, (position_2 + step) % size * span, from_right.shape[0], axis=0
+                ),
+                from_right,
+                preferred_element_type=jnp.float32,
+            )
+        down_total = down_total + jnp.einsum(
+            "rf,rd->fd",
+            lax.dynamic_slice_in_dim(
+                hidden, (position_2 - step) % size * span, from_left.shape[0], axis=0
+            ),
+            from_left,
+            preferred_element_type=jnp.float32,
+        )
     return (down_total.astype(jnp.bfloat16)[None], key_value_grad)
 
 

time: 633 us -> 578 us (0.913)
  waiting for transfers between devices: 435 us -> 326 us
  starting transfers between devices: 7.63 us -> 66.2 us
  blocking collectives: 114 us -> 101 us
  matrix products: 5.81 us -> 13.9 us
    all_gather x1 -> x0, waiting for transfers between devices: 71.5 us -> none  [per_device(): lax.all_gather(landed, 'dp', axis=0, tiled=True)]
    unnamed x7 -> x6, waiting for transfers between devices: 190 us -> 135 us
    ppermute x0 -> x15, starting transfers between devices: none -> 52.5 us  [the longest x7 37.2 us: per_device(): from_right = lax.ppermute(from_right, 'dp', downward)]
    all_to_all x1 -> x0, blocking collectives: 12.6 us -> none  [per_device(): lax.all_to_all(grad_slots, 'expert', split_axis=0, concat_axis=2, tiled=T...]
    ppermute x0 -> x15, waiting for transfers between devices: none -> 12.1 us  [the longest x8 12 us: per_device(): from_left = lax.ppermute(from_left, 'dp', upward)]
    dot_general x1 -> x16, matrix products: 1.43 us -> 8.49 us  [the longest x8 4.71 us: per_device(): jnp.einsum('rf,rd->fd', lax.dynamic_slice_in_dim(hidden, (position_2 - st...]
  transfers between devices with their start and end apart: 6 -> 21, of which waited for: 6 -> 12; matrix products, arithmetic and copies ran while one was open for 1% -> 2% of each run, Pallas kernels for 0% -> 0%
where the time goes in v1:
time: 578 us; the launch traced here: 577 us
  waiting for transfers between devices  326 us (56%)
  blocking collectives  101 us (17%)
  starting transfers between devices  66.2 us (11%)
  other arithmetic  29.4 us (5%)
  local copies, waits for them, and re-layouts  24.1 us (4%)
  between operations  15.4 us (3%)
  matrix products  13.9 us (2%)
    unnamed x6, waiting for transfers between devices  135 us
    reduce_scatter x1, waiting for transfers between devices, per_device(): lax.psum_scatter(proj_term.astype(jnp.bfloat16), 'expert', scatter_dimens...  93.3 us
    all_gather x1, waiting for transfers between devices, per_device(): rows = lax.all_gather(arrived, 'dp', axis=0, tiled=True)  74.2 us
    psum x1, blocking collectives, per_device(): total_sq = lax.psum(jnp.sum(values * values, axis=1), 'expert')  63 us
    ppermute x7, starting transfers between devices, per_device(): from_right = lax.ppermute(from_right, 'dp', downward)  37.2 us
    unnamed x1, other arithmetic  23.4 us
    all_gather x1, blocking collectives, per_device(): cotangent = lax.all_gather(cotangent_cols, 'expert', axis=1, tiled=True)  23.1 us
    ppermute x8, starting transfers between devices, per_device(): from_left = lax.ppermute(from_left, 'dp', upward)  15.3 us
  transfers between devices with their start and end apart: 21, of which 12 were waited for; matrix products, arithmetic and copies ran while one was open for 2% of the time, Pallas kernels for 0%

profile of v1, /device:TPU:2, one launch (start us, length us, event | category | flops | bytes accessed | tf_op | source)
XLA Modules:
  0.0 576.6 jit_solution(6795519435441768480)
XLA Ops:
  7.2 0.9 copy.34
  8.4 0.7 broadcast_multiply_fusion
  9.1 0.9 fusion.14
  9.9 63.0 %psum.7 = f32[128]{0:T(128)S(1)} all-reduce(f32[128]{0:T(128)S(1)} %fusion.14), channel_id=1, replica_groups=mesh['dp'=16,'expert'=32] {'expert'}, use_global_device_ids=true, to_apply=%region_4.5 | all-reduce | flops 128 | bytes 1024 | tf_op jit(solution)/shard_map/psum | solution.py:43
  72.9 0.6 reduce-window.6
  74.0 0.8 dynamic_slice.51
  74.8 0.8 fusion.16
  75.8 1.2 scatter_custom_fusion
  77.0 15.1 %all_to_all.45 = bf16[32,10,128]{2,1,0:T(8,128)(2,1)S(1)} all-to-all(bf16[32,10,128]{2,1,0:T(8,128)(2,1)S(1)} %reshape.83), channel_id=1, replica_groups=mesh['dp'=16,'expert'=32] {'expert'}, dimensions={0} | all-to-all | bytes 163840 | tf_op jit(solution)/shard_map/all_to_all | solution.py:48
  92.1 0.7 reshape.112
  92.9 74.2 %all-gather.3.cloned.1.call-done = bf16[16,10,4096]{2,1,0:T(8,128)(2,1)} async-done(((bf16[1,10,4096]{2,1,0:T(8,128)(2,1)}), bf16[16,10,4096]{2,1,0:T(8,128)(2,1)}) %all-gather.3.cloned.1.call-update) | async-done | bytes 1310736 | tf_op jit(solution)/shard_map/all_gather | solution.py:49
  167.1 1.8 reshape.113
  168.9 0.5 fusion.11
  169.4 0.7 copy-done.3
  170.1 0.5 fusion.8
  170.6 1.6 convolution_convert_fusion
  172.4 1.3 dynamic-slice
  174.3 135.3 %all-reduce.3.cloned.1.call-done = bf16[160,4096]{1,0:T(8,128)(2,1)} async-done(((bf16[160,4096]{1,0:T(8,128)(2,1)}), bf16[160,4096]{1,0:T(8,128)(2,1)}) %all-reduce.3.cloned.1.call-update) | async-done | bytes 1310736
  309.6 1.0 dynamic-slice_bitcast_fusion
  310.5 2.8 copy.38
  313.4 0.5 broadcast.89
  313.9 23.4 %reduce.2 = bf16[4096,10]{1,0:T(8,128)(2,1)} reduce(bf16[4096,1,10]{2,1,0:T(2,128)(2,1)S(1)} %bitcast.90, bf16[]{:T(256)} %broadcast.89), dimensions={1}, to_apply=%bitcast.63.reduce_sub_computation | reduce | bytes 163842
  337.3 3.4 reshape.123
  340.7 7.4 %all-to-all-start.1 = ((bf16[32,2,640]{2,1,0:T(2,128)(2,1)}), bf16[32,2,640]{2,1,0:T(2,128)(2,1)S(1)}, u32[]{:S(2)}, u32[]{:S(2)}) async-start(bf16[32,2,640]{2,1,0:T(2,128)(2,1)} %reshape.123), calls=%async_computation.1 | async-start | bytes 163840 | tf_op jit(solution)/shard_map/all_to_all | solution.py:59
  348.2 6.3 %all-to-all-done.1 = bf16[32,2,640]{2,1,0:T(2,128)(2,1)S(1)} async-done(((bf16[32,2,640]{2,1,0:T(2,128)(2,1)}), bf16[32,2,640]{2,1,0:T(2,128)(2,1)S(1)}, u32[]{:S(2)}, u32[]{:S(2)}) %all-to-all-start.1) | async-done | bytes 81952 | tf_op jit(solution)/shard_map/all_to_all | solution.py:59
  354.4 2.2 reshape.124
  356.7 2.1 copy.39
  359.0 0.9 gather_fusion
  360.1 2.2 convolution_convert_fusion.2
  362.8 93.3 %reduce-scatter.5.cloned.1.call-done = bf16[128,64]{0,1:T(8,128)(2,1)} async-done(((bf16[128,2048]{0,1:T(8,128)(2,1)}), bf16[128,64]{0,1:T(8,128)(2,1)}) %reduce-scatter.5.cloned.1.call-update) | async-done | bytes 16400 | tf_op jit(solution)/shard_map/reduce_scatter | solution.py:64
  456.1 0.7 multiply_convert_fusion.2
  456.9 23.1 %all_gather.7 = bf16[128,2048]{0,1:T(8,128)(2,1)S(1)} all-gather(bf16[128,64]{0,1:T(8,128)(2,1)S(1)} %multiply_convert_fusion.2), channel_id=1, replica_groups=mesh['dp'=16,'expert'=32] {'expert'}, dimensions={1}, use_global_device_ids=true | all-gather | bytes 540672 | tf_op jit(solution)/shard_map/all_gather | solution.py:71
  480.4 1.3 scatter_custom_fusion.1
  481.7 0.7 reshape.86
  482.4 6.1 %all-to-all-start.2 = ((bf16[32,10,128]{2,1,0:T(8,128)(2,1)}), bf16[32,10,128]{2,1,0:T(8,128)(2,1)S(1)}, u32[]{:S(2)}, u32[]{:S(2)}) async-start(bf16[32,10,128]{2,1,0:T(8,128)(2,1)} %reshape.86), calls=%async_computation.3 | async-start | bytes 262144 | tf_op jit(solution)/shard_map/all_to_all | solution.py:83
  488.9 1.0 copy.44
  489.9 5.2 all-to-all-done.2
  495.2 6.0 %collective-permute-start = (bf16[10,4096]{1,0:T(8,128)(2,1)S(1)}, bf16[10,4096]{1,0:T(8,128)(2,1)S(1)}, u32[]{:S(2)}, u32[]{:S(2)}) collective-permute-start(bf16[10,4096]{1,0:T(8,128)(2,1)S(1)} %bitcast.93), channel_id=1, source_target_pairs={{0,480},{32,0},{64,32},{96,64},{128,96},{160,128},{192,160},{224,1... | collective-permute-start | bytes 245768 | tf_op jit(solution)/shard_map/ppermute | solution.py:98
  501.2 1.9 collective-permute-start.1
  503.1 0.5 fusion.48
  503.6 6.0 %collective-permute-done.1 = bf16[10,4096]{1,0:T(8,128)(2,1)S(1)} collective-permute-done((bf16[10,4096]{1,0:T(8,128)(2,1)S(1)}, bf16[10,4096]{1,0:T(8,128)(2,1)S(1)}, u32[]{:S(2)}, u32[]{:S(2)}) %collective-permute-start.1) | collective-permute-done | bytes 81952 | tf_op jit(solution)/shard_map/ppermute | solution.py:96
  509.6 1.9 collective-permute-start.3
  511.5 5.1 collective-permute-start.2
  517.9 1.9 collective-permute-start.5
  519.8 0.5 fusion.43
  520.3 5.1 collective-permute-start.4
  525.5 0.5 fusion.5
  526.2 1.9 collective-permute-start.7
  528.1 0.5 fusion.40
  528.6 5.1 collective-permute-start.6
  533.7 0.5 fusion.4
  534.3 1.9 collective-permute-start.9
  536.7 5.4 collective-permute-start.8
  542.1 0.5 fusion.3
  542.6 1.9 collective-permute-start.11
  545.0 5.3 collective-permute-start.10
  550.3 0.5 fusion.2
  550.8 1.9 collective-permute-start.13
  553.2 5.2 collective-permute-start.12
  559.0 1.9 collective-permute-start.14
  561.9 5.2 collective-permute-done.14
  567.1 1.4 fusion.7
  568.5 0.9 copy.45
  569.4 0.6 convert_element_type.74
  (74 shorter events, 7.3 us)
Async XLA Ops:
  7.2 163.4 %copy-start = (bf16[1,128,4096]{2,1,0:T(8,128)(2,1)S(1)}, bf16[1,128,4096]{2,1,0:T(8,128)(2,1)}, u32[]{:S(2)}) copy-start(bf16[1,128,4096]{2,1,0:T(8,128)(2,1)} %param.16) | copy-start | bytes 3145732
  7.2 159.9 %all-gather.3.cloned.1.call-start = ((), (), s32[]{:S(2)}) async-start(), calls=%async_computation.6 | async-start | bytes 2228224 | tf_op jit(solution)/shard_map/all_gather | solution.py:49
  77.0 91.8 %copy-start.2 = (bf16[1,4096,128]{2,1,0:T(8,128)(2,1)S(1)}, bf16[1,4096,128]{2,1,0:T(8,128)(2,1)}, u32[]{:S(2)}) copy-start(bf16[1,4096,128]{2,1,0:T(8,128)(2,1)} %param.14) | copy-start | bytes 3145732
  92.9 216.7 %all-reduce.3.cloned.1.call-start = ((), (), s32[]{:S(2)}) async-start(), calls=%async_computation.8 | async-start | bytes 2621440
  168.9 1.2 copy-start.3
  170.6 1.6 copy-start.6
  340.7 13.8 %all-to-all-start.1 = ((bf16[32,2,640]{2,1,0:T(2,128)(2,1)}), bf16[32,2,640]{2,1,0:T(2,128)(2,1)S(1)}, u32[]{:S(2)}, u32[]{:S(2)}) async-start(bf16[32,2,640]{2,1,0:T(2,128)(2,1)} %reshape.123), calls=%async_computation.1 | async-start | bytes 163840 | tf_op jit(solution)/shard_map/all_to_all | solution.py:59
  348.1 108.0 %reduce-scatter.5.cloned.1.call-start = ((), (), s32[]{:S(2)}) async-start(), calls=%async_computation.5 | async-start | bytes 540672 | tf_op jit(solution)/shard_map/reduce_scatter | solution.py:64
  356.7 3.4 copy-start.4
  358.8 3.9 copy-start.7
  358.9 97.3 %copy-start.5 = (bf16[128,64]{0,1:T(8,128)(2,1)S(1)}, bf16[128,64]{0,1:T(8,128)(2,1)}, u32[]{:S(2)}) copy-start(bf16[128,64]{0,1:T(8,128)(2,1)} %param.18) | copy-start | bytes 49156
  358.9 121.1 %copy-start.1 = (bf16[128,2048]{1,0:T(8,128)(2,1)S(1)}, bf16[128,2048]{1,0:T(8,128)(2,1)}, u32[]{:S(2)}) copy-start(bf16[128,2048]{1,0:T(8,128)(2,1)} %param.17) | copy-start | bytes 1572868
  482.4 12.8 %all-to-all-start.2 = ((bf16[32,10,128]{2,1,0:T(8,128)(2,1)}), bf16[32,10,128]{2,1,0:T(8,128)(2,1)S(1)}, u32[]{:S(2)}, u32[]{:S(2)}) async-start(bf16[32,10,128]{2,1,0:T(8,128)(2,1)} %reshape.86), calls=%async_computation.3 | async-start | bytes 262144 | tf_op jit(solution)/shard_map/all_to_all | solution.py:83
  488.5 80.0 %reduce-scatter.7.cloned.1.call-start = ((), (), s32[]{:S(2)}) async-start(), calls=%async_computation.7 | async-start | bytes 557056
  495.2 16.3 %collective-permute-start = (bf16[10,4096]{1,0:T(8,128)(2,1)S(1)}, bf16[10,4096]{1,0:T(8,128)(2,1)S(1)}, u32[]{:S(2)}, u32[]{:S(2)}) collective-permute-start(bf16[10,4096]{1,0:T(8,128)(2,1)S(1)} %bitcast.93), channel_id=1, source_target_pairs={{0,480},{32,0},{64,32},{96,64},{128,96},{160,128},{192,160},{224,1... | collective-permute-start | bytes 245768 | tf_op jit(solution)/shard_map/ppermute | solution.py:98
  501.2 8.4 %collective-permute-start.1 = (bf16[10,4096]{1,0:T(8,128)(2,1)S(1)}, bf16[10,4096]{1,0:T(8,128)(2,1)S(1)}, u32[]{:S(2)}, u32[]{:S(2)}) collective-permute-start(bf16[10,4096]{1,0:T(8,128)(2,1)S(1)} %bitcast.94), channel_id=1, source_target_pairs={{0,32},{32,64},{64,96},{96,128},{128,160},{160,192},{192,224},{224... | collective-permute-start | bytes 245768 | tf_op jit(solution)/shard_map/ppermute | solution.py:96
  509.6 8.3 %collective-permute-start.3 = (bf16[10,4096]{1,0:T(8,128)(2,1)S(1)}, bf16[10,4096]{1,0:T(8,128)(2,1)S(1)}, u32[]{:S(2)}, u32[]{:S(2)}) collective-permute-start(bf16[10,4096]{1,0:T(8,128)(2,1)S(1)} %collective-permute-done.1), channel_id=1, source_target_pairs={{0,32},{32,64},{64,96},{96,128},{128,160},{160,192},{192,224},{224... | collective-permute-start | bytes 245768 | tf_op jit(solution)/shard_map/ppermute | solution.py:96
  511.5 8.8 %collective-permute-start.2 = (bf16[10,4096]{1,0:T(8,128)(2,1)S(1)}, bf16[10,4096]{1,0:T(8,128)(2,1)S(1)}, u32[]{:S(2)}, u32[]{:S(2)}) collective-permute-start(bf16[10,4096]{1,0:T(8,128)(2,1)S(1)} %collective-permute-done), channel_id=1, source_target_pairs={{0,480},{32,0},{64,32},{96,64},{128,96},{160,128},{192,160},{224,1... | collective-permute-start | bytes 245768 | tf_op jit(solution)/shard_map/ppermute | solution.py:98
  517.9 8.2 %collective-permute-start.5 = (bf16[10,4096]{1,0:T(8,128)(2,1)S(1)}, bf16[10,4096]{1,0:T(8,128)(2,1)S(1)}, u32[]{:S(2)}, u32[]{:S(2)}) collective-permute-start(bf16[10,4096]{1,0:T(8,128)(2,1)S(1)} %collective-permute-done.3), channel_id=1, source_target_pairs={{0,32},{32,64},{64,96},{96,128},{128,160},{160,192},{192,224},{224... | collective-permute-start | bytes 245768 | tf_op jit(solution)/shard_map/ppermute | solution.py:96
  520.3 8.2 %collective-permute-start.4 = (bf16[10,4096]{1,0:T(8,128)(2,1)S(1)}, bf16[10,4096]{1,0:T(8,128)(2,1)S(1)}, u32[]{:S(2)}, u32[]{:S(2)}) collective-permute-start(bf16[10,4096]{1,0:T(8,128)(2,1)S(1)} %collective-permute-done.2), channel_id=1, source_target_pairs={{0,480},{32,0},{64,32},{96,64},{128,96},{160,128},{192,160},{224,1... | collective-permute-start | bytes 245768 | tf_op jit(solution)/shard_map/ppermute | solution.py:98
  526.2 8.1 %collective-permute-start.7 = (bf16[10,4096]{1,0:T(8,128)(2,1)S(1)}, bf16[10,4096]{1,0:T(8,128)(2,1)S(1)}, u32[]{:S(2)}, u32[]{:S(2)}) collective-permute-start(bf16[10,4096]{1,0:T(8,128)(2,1)S(1)} %collective-permute-done.5), channel_id=1, source_target_pairs={{0,32},{32,64},{64,96},{96,128},{128,160},{160,192},{192,224},{224... | collective-permute-start | bytes 245768 | tf_op jit(solution)/shard_map/ppermute | solution.py:96
  528.6 8.1 %collective-permute-start.6 = (bf16[10,4096]{1,0:T(8,128)(2,1)S(1)}, bf16[10,4096]{1,0:T(8,128)(2,1)S(1)}, u32[]{:S(2)}, u32[]{:S(2)}) collective-permute-start(bf16[10,4096]{1,0:T(8,128)(2,1)S(1)} %collective-permute-done.4), channel_id=1, source_target_pairs={{0,480},{32,0},{64,32},{96,64},{128,96},{160,128},{192,160},{224,1... | collective-permute-start | bytes 245768 | tf_op jit(solution)/shard_map/ppermute | solution.py:98
  534.3 8.3 %collective-permute-start.9 = (bf16[10,4096]{1,0:T(8,128)(2,1)S(1)}, bf16[10,4096]{1,0:T(8,128)(2,1)S(1)}, u32[]{:S(2)}, u32[]{:S(2)}) collective-permute-start(bf16[10,4096]{1,0:T(8,128)(2,1)S(1)} %collective-permute-done.7), channel_id=1, source_target_pairs={{0,32},{32,64},{64,96},{96,128},{128,160},{160,192},{192,224},{224... | collective-permute-start | bytes 245768 | tf_op jit(solution)/shard_map/ppermute | solution.py:96
  536.7 8.3 %collective-permute-start.8 = (bf16[10,4096]{1,0:T(8,128)(2,1)S(1)}, bf16[10,4096]{1,0:T(8,128)(2,1)S(1)}, u32[]{:S(2)}, u32[]{:S(2)}) collective-permute-start(bf16[10,4096]{1,0:T(8,128)(2,1)S(1)} %collective-permute-done.6), channel_id=1, source_target_pairs={{0,480},{32,0},{64,32},{96,64},{128,96},{160,128},{192,160},{224,1... | collective-permute-start | bytes 245768 | tf_op jit(solution)/shard_map/ppermute | solution.py:98
  542.6 8.2 %collective-permute-start.11 = (bf16[10,4096]{1,0:T(8,128)(2,1)S(1)}, bf16[10,4096]{1,0:T(8,128)(2,1)S(1)}, u32[]{:S(2)}, u32[]{:S(2)}) collective-permute-start(bf16[10,4096]{1,0:T(8,128)(2,1)S(1)} %collective-permute-done.9), channel_id=1, source_target_pairs={{0,32},{32,64},{64,96},{96,128},{128,160},{160,192},{192,224},{224... | collective-permute-start | bytes 245768 | tf_op jit(solution)/shard_map/ppermute | solution.py:96
  545.0 8.2 %collective-permute-start.10 = (bf16[10,4096]{1,0:T(8,128)(2,1)S(1)}, bf16[10,4096]{1,0:T(8,128)(2,1)S(1)}, u32[]{:S(2)}, u32[]{:S(2)}) collective-permute-start(bf16[10,4096]{1,0:T(8,128)(2,1)S(1)} %collective-permute-done.8), channel_id=1, source_target_pairs={{0,480},{32,0},{64,32},{96,64},{128,96},{160,128},{192,160},{224,1... | collective-permute-start | bytes 245768 | tf_op jit(solution)/shard_map/ppermute | solution.py:98
  550.8 8.2 %collective-permute-start.13 = (bf16[10,4096]{1,0:T(8,128)(2,1)S(1)}, bf16[10,4096]{1,0:T(8,128)(2,1)S(1)}, u32[]{:S(2)}, u32[]{:S(2)}) collective-permute-start(bf16[10,4096]{1,0:T(8,128)(2,1)S(1)} %collective-permute-done.11), channel_id=1, source_target_pairs={{0,32},{32,64},{64,96},{96,128},{128,160},{160,192},{192,224},{224... | collective-permute-start | bytes 245768 | tf_op jit(solution)/shard_map/ppermute | solution.py:96
  553.2 8.2 %collective-permute-start.12 = (bf16[10,4096]{1,0:T(8,128)(2,1)S(1)}, bf16[10,4096]{1,0:T(8,128)(2,1)S(1)}, u32[]{:S(2)}, u32[]{:S(2)}) collective-permute-start(bf16[10,4096]{1,0:T(8,128)(2,1)S(1)} %collective-permute-done.10), channel_id=1, source_target_pairs={{0,480},{32,0},{64,32},{96,64},{128,96},{160,128},{192,160},{224,1... | collective-permute-start | bytes 245768 | tf_op jit(solution)/shard_map/ppermute | solution.py:98
  559.0 8.1 %collective-permute-start.14 = (bf16[10,4096]{1,0:T(8,128)(2,1)S(1)}, bf16[10,4096]{1,0:T(8,128)(2,1)S(1)}, u32[]{:S(2)}, u32[]{:S(2)}) collective-permute-start(bf16[10,4096]{1,0:T(8,128)(2,1)S(1)} %collective-permute-done.13), channel_id=1, source_target_pairs={{0,32},{32,64},{64,96},{96,128},{128,160},{160,192},{192,224},{224... | collective-permute-start | bytes 245768 | tf_op jit(solution)/shard_map/ppermute | solution.py:96
Sparse Core Ops, SparseCore 0:
  93.0 74.0 all-gather.2
  172.4 137.1 all-reduce.2
  362.5 93.6 reduce-scatter.4
  491.8 70.9 reduce-scatter.6
